TPU v7x, 32 devices: a whole 2x2x4 slice. The times are simulated.
32 devices in a mesh: phase: 2 (over x), expert: 4 (over y, core), tensor: 4 (over z).
Axes of the slice: x: 2, y: 2, z: 4, core: 2. Of those that a mesh axis runs over, the one named last changes fastest.
Arguments:
- forward_routes: int32 [2, 256, 6], P('phase', 'expert'), may hold values from 0 to 11, all different within a row; in each aligned block of 64 rows (0 to 63, 64 to 127, ..., all dimensions but the last counted through in order) at most 43 rows name the same one
- forward_gates: float32 [2, 256, 6], P('phase', 'expert'), may hold values from 0.05 to 1
- hidden_rows: bfloat16 [2, 12, 4, 43, 1024], P('phase', 'expert', None, None, 'tensor'), may hold values from -6 to 6
- down_weight: bfloat16 [2, 12, 1024, 2560], P('phase', 'expert', 'tensor'), may hold values from -0.1875 to 0.1875
- shared_hidden: bfloat16 [2, 256, 1536], P('phase', 'expert', 'tensor'), may hold values from -6 to 6
- shared_weight: bfloat16 [2, 1536, 2560], P('phase', 'tensor', 'expert'), may hold values from -0.15625 to 0.15625
- backward_routes: int32 [2, 256, 6], P('phase', 'expert'), may hold values from 0 to 11, all different within a row; in each aligned block of 64 rows (0 to 63, 64 to 127, ..., all dimensions but the last counted through in order) at most 43 rows name the same one
- backward_gates: float32 [2, 256, 6], P('phase', 'expert'), may hold values from 0.05 to 1
- cotangent: bfloat16 [2, 256, 2560], P('phase', 'expert', 'tensor'), may hold values from -6 to 6
Outputs:
- forward_next: bfloat16 [2, 256, 2560], P('phase', 'expert', 'tensor')
- hidden_grad: bfloat16 [2, 12, 4, 43, 1024], P('phase', 'expert', None, None, 'tensor')
- shared_grad: bfloat16 [2, 256, 1536], P('phase', 'expert', 'tensor')
Inputs may be any that keep to these rules, and one draw needn't show every extreme that they name: `forward_routes`: each token names 6 different experts. The tokens of one token group (the 64 rows of one device) name any one expert 43 times at most, and some group reaches that. `backward_routes`: as for forward_routes.
All inputs are finite; a program needn't handle non-finite values.
Results may differ from a plain program's by a relative error of at most 0.0049.
Values may be sent and summed in bfloat16 or wider, within the bound.
A program may use at most 64 MiB of HBM per device.

v0:
```python
import jax
import jax.numpy as jnp
from jax import lax
from jax.sharding import PartitionSpec as P


def shifted(value, axis, steps):
    count = lax.axis_size(axis)
    pairs = [(source, (source + steps) % count) for source in range(count)]
    return lax.ppermute(value, axis, pairs)


def slot_numbers(routes, experts):
    numbers = jnp.arange(experts, dtype=jnp.int32)
    onehot = (routes[:, :, None] == numbers[None, None, :]).astype(jnp.int32)
    per_token = jnp.sum(onehot, axis=1)
    before = jnp.cumsum(per_token, axis=0) - per_token
    return jnp.sum(onehot * before[:, None, :], axis=2)


def row_positions(routes, experts_here, groups, capacity):
    slot_index = slot_numbers(routes, experts_here * groups)
    holder = routes // experts_here
    within = routes - holder * experts_here
    return ((within * groups + holder) * capacity + slot_index).reshape(-1)


def place_rows(gates, values, positions, total_rows):
    scaled = (gates[:, :, None] * values[:, None, :].astype(jnp.float32)).astype(jnp.bfloat16)
    outgoing = jnp.zeros((total_rows, values.shape[1]), jnp.bfloat16)
    return outgoing.at[positions].set(scaled.reshape(-1, values.shape[1]))


def on_device(
    forward_routes,
    forward_gates,
    hidden_rows,
    down_weight,
    shared_hidden,
    shared_weight,
    backward_routes,
    backward_gates,
    cotangent,
):
    experts_here = down_weight.shape[1]
    features = down_weight.shape[3]
    capacity = hidden_rows.shape[3]
    groups = lax.axis_size("expert")
    token_count = forward_routes.shape[1]
    top_count = forward_routes.shape[2]
    hidden = hidden_rows[0]
    weight = down_weight[0]
    local_shared = shared_hidden[0]
    shared_piece = shared_weight[0]
    shared_part = jnp.dot(
        local_shared,
        lax.all_gather(shared_piece, "expert", axis=1, tiled=True),
        preferred_element_type=jnp.float32,
    )
    fore_positions = row_positions(forward_routes[0], experts_here, groups, capacity)
    fore_gates = forward_gates[0]
    partial_value = jnp.einsum(
        "egmh,ehd->egmd", hidden, weight, preferred_element_type=jnp.float32
    ).astype(jnp.bfloat16)
    arrived = lax.all_to_all(partial_value, "expert", split_axis=1, concat_axis=1, tiled=True)
    picked = arrived.reshape(-1, features)[fore_positions].reshape(token_count, top_count, features)
    summand = shared_part + jnp.sum(picked.astype(jnp.float32) * fore_gates[:, :, None], axis=1)
    summed = lax.psum_scatter(summand, "tensor", scatter_dimension=1, tiled=True)
    layer_out = summed.astype(jnp.bfloat16)
    handed = shifted(layer_out, "phase", 1)
    cotangent_whole = lax.all_gather(cotangent[0], "tensor", axis=1, tiled=True)
    back_positions = row_positions(backward_routes[0], experts_here, groups, capacity)
    total_rows = experts_here * groups * capacity
    outgoing = place_rows(backward_gates[0], cotangent_whole, back_positions, total_rows)
    received = lax.all_to_all(
        outgoing.reshape(experts_here, groups, capacity, features),
        "expert",
        split_axis=1,
        concat_axis=1,
        tiled=True,
    )
    hidden_back = jnp.einsum(
        "egmd,ehd->egmh", received, weight, preferred_element_type=jnp.float32
    ).astype(jnp.bfloat16)
    shared_back = lax.dot_general(
        cotangent_whole,
        lax.all_gather(shared_piece, "expert", axis=1, tiled=True),
        (((1,), (1,)), ((), ())),
        preferred_element_type=jnp.float32,
    )
    return (handed[None], hidden_back[None], shared_back.astype(jnp.bfloat16)[None])


def solution(mesh):
    return jax.shard_map(
        on_device,
        mesh=mesh,
        in_specs=(
            P("phase", "expert", None),
            P("phase", "expert", None),
            P("phase", "expert", None, None, "tensor"),
            P("phase", "expert", "tensor", None),
            P("phase", "expert", "tensor"),
            P("phase", "tensor", "expert"),
            P("phase", "expert", None),
            P("phase", "expert", None),
            P("phase", "expert", "tensor"),
        ),
        out_specs=(
            P("phase", "expert", "tensor"),
            P("phase", "expert", None, None, "tensor"),
            P("phase", "expert", "tensor"),
        ),
        check_vma=False,
    )
```

profile of v0, /device:TPU:0, one launch (start us, length us, event | category | flops | bytes accessed | tf_op | source)
XLA Modules:
  0.0 125.8 jit_solution(11114866038983174019)
XLA Ops:
  7.9 3.2 %convolution_convert_fusion = bf16[3,4,43,2560]{3,2,1,0:T(8,128)(2,1)S(1)} fusion(bf16[1,3,256,2560]{3,2,1,0:T(8,128)(2,1)} %param.12, bf16[3,4,43,256]{3,1,2,0:T(4,128)(2,1)} %bitcast.42), kind=kOutput, calls=%fused_computation.3 | convolution fusion | flops 677652480 | bytes 6838272 | tf_op jit(solution)/shard_map/egmh,ehd->egmd/dot_general | solution.py:62
  11.1 1.8 %copy.38 = bf16[3,4,43,2560]{3,2,0,1:T(8,128)(2,1)} copy(bf16[3,4,43,2560]{3,2,1,0:T(8,128)(2,1)S(1)} %convolution_convert_fusion) | data formatting | bytes 5283840 | tf_op jit(solution)/shard_map/convert_element_type | solution.py:64
  12.8 4.4 %all-to-all-start = ((bf16[3,4,43,2560]{3,2,0,1:T(8,128)(2,1)}), bf16[3,4,43,2560]{3,2,0,1:T(8,128)(2,1)S(1)}, u32[]{:S(2)}, u32[]{:S(2)}) async-start(bf16[3,4,43,2560]{3,2,0,1:T(8,128)(2,1)} %copy.38), calls=%async_computation | async-start | bytes 5898240 | tf_op jit(solution)/shard_map/all_to_all | solution.py:65
  18.3 15.6 %all-gather.1 = bf16[1,64,2560]{2,1,0:T(8,128)(2,1)S(1)} all-gather(bf16[1,64,640]{2,1,0:T(8,128)(2,1)S(1)} %copy-done.2), channel_id=3, replica_groups=mesh['phase'=2,'expert'=4,'tensor'=4] {'tensor'}, dimensions={2}, use_global_device_ids=true | all-gather | bytes 409600 | tf_op jit(solution)/shard_map/all_gather | solution.py:71
  33.9 3.0 %mul.125 = f32[64,6,2560]{2,1,0:T(8,128)} broadcast(f32[64,2560]{1,0:T(8,128)S(1)} %bitcast_convert_fusion), dimensions={0,2} | broadcast | bytes 4587520 | tf_op jit(solution)/shard_map/mul | solution.py:29
  36.9 5.1 %mul.126 = f32[384,2560]{1,0:T(8,128)} reshape(f32[64,6,2560]{2,1,0:T(8,128)} %mul.125) | data formatting | bytes 7864320 | tf_op jit(solution)/shard_map/mul | solution.py:29
  42.0 6.8 %scatter_custom_fusion = bf16[516,2560]{1,0:T(8,128)(2,1)} fusion(s32[384]{0:T(512)S(1)} %fusion.30, f32[384,2560]{1,0:T(8,128)} %mul.126, f32[384]{0:T(512)S(1)} %mul.123, bf16[]{:T(256)} %constant.32.clone.1), kind=kCustom, calls=%fused_computation.10 | custom fusion | flops 1966080 | bytes 6576130 | tf_op jit(solution)/shard_map/scatter | solution.py:31
  48.9 3.6 %reshape.216 = bf16[3,4,43,2560]{3,2,1,0:T(8,128)(2,1)} reshape(bf16[516,2560]{1,0:T(8,128)(2,1)} %scatter_custom_fusion) | data formatting | bytes 5283840 | tf_op jit(solution)/shard_map/reshape | solution.py:76
  52.5 3.6 %copy.52 = bf16[3,4,43,2560]{3,2,0,1:T(8,128)(2,1)} copy(bf16[3,4,43,2560]{3,2,1,0:T(8,128)(2,1)} %reshape.216) | data formatting | bytes 5283840 | tf_op jit(solution)/shard_map/reshape | solution.py:76
  56.1 6.5 %all-to-all-done = bf16[3,4,43,2560]{3,2,0,1:T(8,128)(2,1)S(1)} async-done(((bf16[3,4,43,2560]{3,2,0,1:T(8,128)(2,1)}), bf16[3,4,43,2560]{3,2,0,1:T(8,128)(2,1)S(1)}, u32[]{:S(2)}, u32[]{:S(2)}) %all-to-all-start) | async-done | bytes 2641952 | tf_op jit(solution)/shard_map/all_to_all | solution.py:65
  62.6 4.7 %all-to-all-start.1 = ((bf16[3,4,43,2560]{3,2,0,1:T(8,128)(2,1)}), bf16[3,4,43,2560]{3,2,0,1:T(8,128)(2,1)}, u32[]{:S(2)}, u32[]{:S(2)}) async-start(bf16[3,4,43,2560]{3,2,0,1:T(8,128)(2,1)} %copy.52), calls=%async_computation.2 | async-start | bytes 5898240 | tf_op jit(solution)/shard_map/all_to_all | solution.py:75
  68.5 1.8 %copy.39 = bf16[3,4,43,2560]{3,2,1,0:T(8,128)(2,1)} copy(bf16[3,4,43,2560]{3,2,0,1:T(8,128)(2,1)S(1)} %all-to-all-done) | data formatting | bytes 5283840 | tf_op jit(solution)/shard_map/all_to_all | solution.py:65
  70.4 2.4 %reshape.215 = bf16[516,2560]{1,0:T(8,128)(2,1)S(1)} reshape(bf16[3,4,43,2560]{3,2,1,0:T(8,128)(2,1)} %copy.39) | data formatting | bytes 5283840 | tf_op jit(solution)/shard_map/reshape | solution.py:66
  72.8 3.3 %gather_fusion = bf16[384,2560]{1,0:T(8,128)(2,1)} fusion(bf16[516,2560]{1,0:T(8,128)(2,1)S(1)} %reshape.215, s32[1024]{0:T(1024)S(1)} %pad_clamp_fusion), kind=kCustom, calls=%fused_computation | custom fusion | bytes 3933696 | tf_op jit(solution)/shard_map/gather | solution.py:66
  76.1 4.5 %reshape.217 = f32[64,6,2560]{2,1,0:T(8,128)} reshape(bf16[384,2560]{1,0:T(8,128)(2,1)} %gather_fusion) | data formatting | bytes 5898240 | tf_op jit(solution)/shard_map/convert_element_type | solution.py:67
  80.5 4.4 %multiply_reduce_fusion = f32[64,2560]{1,0:T(8,128)S(1)} fusion(f32[64,6,2560]{2,1,0:T(8,128)} %reshape.217, f32[64,6]{1,0:T(8,128)S(1)} %bitcast.43), kind=kLoop, calls=%fused_computation.2 | loop fusion | flops 1802240 | bytes 4589056 | tf_op jit(solution)/shard_map/reduce_sum | solution.py:67
  85.0 2.9 %convolution_add_fusion = f32[64,2560]{1,0:T(8,128)} fusion(f32[64,2560]{1,0:T(8,128)S(1)} %multiply_reduce_fusion, bf16[1,384,2560]{2,1,0:T(8,128)(2,1)} %all-gather.4.cloned.1.call-done, bf16[1,64,384]{2,1,0:T(8,128)(2,1)S(1)} %copy-done), kind=kOutput, calls=%fused_computation.8 | convolution fusion | flops 125992960 | bytes 3325952 | tf_op jit(solution)/shard_map/dot_general | solution.py:55
  87.9 14.3 %all-to-all-done.1 = bf16[3,4,43,2560]{3,2,0,1:T(8,128)(2,1)} async-done(((bf16[3,4,43,2560]{3,2,0,1:T(8,128)(2,1)}), bf16[3,4,43,2560]{3,2,0,1:T(8,128)(2,1)}, u32[]{:S(2)}, u32[]{:S(2)}) %all-to-all-start.1) | async-done | bytes 2641952 | tf_op jit(solution)/shard_map/all_to_all | solution.py:75
  102.2 4.5 %fusion.15 = bf16[1,3,4,43,256]{4,3,2,1,0:T(8,128)(2,1)S(1)} fusion(bf16[1,3,256,2560]{3,2,1,0:T(8,128)(2,1)} %param.12, bf16[3,4,43,2560]{3,2,0,1:T(8,128)(2,1)} %all-to-all-done.1), kind=kOutput, calls=%fused_computation.17 | convolution fusion | flops 676463616 | bytes 6838272 | tf_op jit(solution)/shard_map/egmd,ehd->egmh/dot_general | solution.py:82
  107.5 5.3 %reduce-scatter.2.cloned.1.call-done = f32[64,640]{1,0:T(8,128)} async-done(((f32[64,2560]{1,0:T(8,128)}), f32[64,640]{1,0:T(8,128)}) %reduce-scatter.2.cloned.1.call-update) | async-done | bytes 163856 | tf_op jit(solution)/shard_map/reduce_scatter | solution.py:68
  112.8 0.9 convert_element_type.36
  113.8 1.5 %collective-permute-start = (bf16[64,640]{1,0:T(8,128)(2,1)S(1)}, bf16[64,640]{1,0:T(8,128)(2,1)S(1)}, u32[]{:S(2)}, u32[]{:S(2)}) collective-permute-start(bf16[64,640]{1,0:T(8,128)(2,1)S(1)} %convert_element_type.36), channel_id=1, source_target_pairs={{0,16},{16,0},{1,17},{17,1},{2,18},{18,2},{3,19},{19,3},{4,20},{20... | collective-permute-start | bytes 245768 | tf_op jit(solution)/shard_map/ppermute | solution.py:10
  115.3 1.4 %fusion.23 = bf16[1,64,384]{2,1,0:T(8,128)(2,1)} fusion(bf16[1,384,2560]{2,1,0:T(8,128)(2,1)S(1)} %copy-done.1, bf16[1,64,2560]{2,1,0:T(8,128)(2,1)S(1)} %all-gather.1), kind=kOutput, calls=%fused_computation.19 | convolution fusion | flops 125853696 | bytes 2342912 | tf_op jit(solution)/shard_map/dot_general | solution.py:85
  116.7 1.6 %collective-permute-done = bf16[64,640]{1,0:T(8,128)(2,1)S(1)} collective-permute-done((bf16[64,640]{1,0:T(8,128)(2,1)S(1)}, bf16[64,640]{1,0:T(8,128)(2,1)S(1)}, u32[]{:S(2)}, u32[]{:S(2)}) %collective-permute-start) | collective-permute-done | bytes 81952 | tf_op jit(solution)/shard_map/ppermute | solution.py:10
  (50 shorter events, 4.5 us)
Async XLA Ops:
  7.2 77.8 %copy-start = (bf16[1,64,384]{2,1,0:T(8,128)(2,1)S(1)}, bf16[1,64,384]{2,1,0:T(8,128)(2,1)}, u32[]{:S(2)}) copy-start(bf16[1,64,384]{2,1,0:T(8,128)(2,1)} %param.13) | copy-start | bytes 147460
  7.2 77.8 %all-gather.4.cloned.1.call-start = ((), (), s32[]{:S(2)}) async-start(), calls=%async_computation.4 | async-start | bytes 2457600 | tf_op jit(solution)/shard_map/all_gather | solution.py:57
  12.8 4.4 %copy-start.3 = (s32[1,64,6]{1,0,2:T(1,128)S(1)}, s32[1,64,6]{1,0,2:T(1,128)}, u32[]{:S(2)}) copy-start(s32[1,64,6]{1,0,2:T(1,128)} %param.15) | copy-start | bytes 4612
  12.8 5.1 %copy-start.5 = (f32[1,64,6]{1,0,2:T(1,128)S(1)}, f32[1,64,6]{1,0,2:T(1,128)}, u32[]{:S(2)}) copy-start(f32[1,64,6]{1,0,2:T(1,128)} %param.16) | copy-start | bytes 4612
  12.8 5.5 %copy-start.2 = (bf16[1,64,640]{2,1,0:T(8,128)(2,1)S(1)}, bf16[1,64,640]{2,1,0:T(8,128)(2,1)}, u32[]{:S(2)}) copy-start(bf16[1,64,640]{2,1,0:T(8,128)(2,1)} %param.17) | copy-start | bytes 245764
  12.8 49.8 %all-to-all-start = ((bf16[3,4,43,2560]{3,2,0,1:T(8,128)(2,1)}), bf16[3,4,43,2560]{3,2,0,1:T(8,128)(2,1)S(1)}, u32[]{:S(2)}, u32[]{:S(2)}) async-start(bf16[3,4,43,2560]{3,2,0,1:T(8,128)(2,1)} %copy.38), calls=%async_computation | async-start | bytes 5898240 | tf_op jit(solution)/shard_map/all_to_all | solution.py:65
  56.1 11.5 %copy-start.4 = (s32[1,64,6]{1,0,2:T(1,128)S(1)}, s32[1,64,6]{1,0,2:T(1,128)}, u32[]{:S(2)}) copy-start(s32[1,64,6]{1,0,2:T(1,128)} %param.9) | copy-start | bytes 4612
  56.1 12.1 %copy-start.6 = (f32[1,64,6]{1,0,2:T(1,128)S(1)}, f32[1,64,6]{1,0,2:T(1,128)}, u32[]{:S(2)}) copy-start(f32[1,64,6]{1,0,2:T(1,128)} %param.10) | copy-start | bytes 4612
  62.6 39.5 %all-to-all-start.1 = ((bf16[3,4,43,2560]{3,2,0,1:T(8,128)(2,1)}), bf16[3,4,43,2560]{3,2,0,1:T(8,128)(2,1)}, u32[]{:S(2)}, u32[]{:S(2)}) async-start(bf16[3,4,43,2560]{3,2,0,1:T(8,128)(2,1)} %copy.52), calls=%async_computation.2 | async-start | bytes 5898240 | tf_op jit(solution)/shard_map/all_to_all | solution.py:75
  67.3 45.5 %reduce-scatter.2.cloned.1.call-start = ((), (), s32[]{:S(2)}) async-start(), calls=%async_computation.3 | async-start | bytes 819200 | tf_op jit(solution)/shard_map/reduce_scatter | solution.py:68
  87.9 27.4 %copy-start.1 = (bf16[1,384,2560]{2,1,0:T(8,128)(2,1)S(1)}, bf16[1,384,2560]{2,1,0:T(8,128)(2,1)}, u32[]{:S(2)}) copy-start(bf16[1,384,2560]{2,1,0:T(8,128)(2,1)} %all-gather.4.cloned.1.call-done) | copy-start | bytes 5898244
  113.8 4.5 %collective-permute-start = (bf16[64,640]{1,0:T(8,128)(2,1)S(1)}, bf16[64,640]{1,0:T(8,128)(2,1)S(1)}, u32[]{:S(2)}, u32[]{:S(2)}) collective-permute-start(bf16[64,640]{1,0:T(8,128)(2,1)S(1)} %convert_element_type.36), channel_id=1, source_target_pairs={{0,16},{16,0},{1,17},{17,1},{2,18},{18,2},{3,19},{19,3},{4,20},{20... | collective-permute-start | bytes 245768 | tf_op jit(solution)/shard_map/ppermute | solution.py:10
Sparse Core Ops, SparseCore 0:
  9.6 35.1 all-gather.3
  88.0 24.8 reduce-scatter.1
where the time goes:
time: 126 us
  local copies, waits for them, and re-layouts  32.2 us (26%)
  waiting for transfers between devices  28.5 us (23%)
  blocking collectives  15.6 us (12%)
  between operations  14.2 us (11%)
  other arithmetic  12.6 us (10%)
  matrix products  11.8 us (9%)
  starting transfers between devices  10.8 us (9%)
    all_gather x1, blocking collectives, on_device(): cotangent_whole = lax.all_gather(cotangent[0], 'tensor', axis=1, tiled=True)  15.6 us
    all_to_all x1, waiting for transfers between devices, on_device(): lax.all_to_all(outgoing.reshape(experts_here, groups, capacity, features)...  14.3 us
    mul x3, local copies, waits for them, and re-layouts, place_rows(): gates[:, :, None] * values[:, None, :].astype(jnp.float32)  8.23 us
    reshape x2, local copies, waits for them, and re-layouts, on_device(): outgoing.reshape(experts_here, groups, capacity, features)  7.22 us
    scatter x1, other arithmetic, place_rows(): return outgoing.at[positions].set(scaled.reshape(-1, values.shape[1]))  6.83 us
    all_to_all x1, waiting for transfers between devices, on_device(): lax.all_to_all(partial_value, 'expert', split_axis=1, concat_axis=1, tile...  6.55 us
    reduce_scatter x1, waiting for transfers between devices, on_device(): lax.psum_scatter(summand, 'tensor', scatter_dimension=1, tiled=True)  5.33 us
    all_to_all x1, starting transfers between devices, on_device(): lax.all_to_all(outgoing.reshape(experts_here, groups, capacity, features)...  4.66 us
  transfers between devices with their start and end apart: 5, of which 4 were waited for; matrix products, arithmetic and copies ran while one was open for 44% of the time, Pallas kernels for 0%

commit v1 on v0

--- a/solution.py
+++ b/solution.py
@@ -68,7 +68,9 @@
     summed = lax.psum_scatter(summand, "tensor", scatter_dimension=1, tiled=True)
     layer_out = summed.astype(jnp.bfloat16)
     handed = shifted(layer_out, "phase", 1)
-    cotangent_whole = lax.all_gather(cotangent[0], "tensor", axis=1, tiled=True)
+    cotangent_whole = jnp.concatenate(
+        lax.all_to_all(jnp.stack([cotangent[0]] * lax.axis_size("tensor")), "tensor", 0, 0), axis=1
+    )
     back_positions = row_positions(backward_routes[0], experts_here, groups, capacity)
     total_rows = experts_here * groups * capacity
     outgoing = place_rows(backward_gates[0], cotangent_whole, back_positions, total_rows)

time: 126 us -> 134 us (1.063)
  blocking collectives: 15.6 us -> 0 us
  waiting for transfers between devices: 28.5 us -> 42 us
  starting transfers between devices: 10.8 us -> 16.4 us
  local copies, waits for them, and re-layouts: 32.2 us -> 36.1 us
    all_gather x1 -> x0, blocking collectives: 15.6 us -> none  [on_device(): cotangent_whole = lax.all_gather(cotangent[0], 'tensor', axis=1, tiled=True)]
    all_to_all x1, waiting for transfers between devices: 6.55 us -> 16.5 us  [on_device(): lax.all_to_all(partial_value, 'expert', split_axis=1, concat_axis=1, tile...]
    all_to_all x0 -> x1, starting transfers between devices: none -> 6.35 us  [on_device(): lax.all_to_all(jnp.stack([cotangent[0]] * lax.axis_size('tensor')), 'tens...]
    all_to_all x0 -> x1, waiting for transfers between devices: none -> 4.65 us  [on_device(): lax.all_to_all(jnp.stack([cotangent[0]] * lax.axis_size('tensor')), 'tens...]
    another operation x0 -> x2, local copies, waits for them, and re-layouts: none -> 2.68 us  [the longest x1 1.67 us: on_device(): jnp.stack([cotangent[0]] * lax.axis_size('tensor'))]
  transfers between devices with their start and end apart: 5 -> 6, of which waited for: 4 -> 5; matrix products, arithmetic and copies ran while one was open for 44% -> 42% of each run, Pallas kernels for 0% -> 0%
where the time goes in v1:
time: 134 us; the launch traced here: 133 us
  waiting for transfers between devices  42 us (31%)
  local copies, waits for them, and re-layouts  36.1 us (27%)
  starting transfers between devices  16.4 us (12%)
  between operations  14.2 us (11%)
  other arithmetic  12.6 us (9%)
  matrix products  11.9 us (9%)
    all_to_all x1, waiting for transfers between devices, on_device(): lax.all_to_all(partial_value, 'expert', split_axis=1, concat_axis=1, tile...  16.5 us
    all_to_all x1, waiting for transfers between devices, on_device(): lax.all_to_all(outgoing.reshape(experts_here, groups, capacity, features)...  14 us
    mul x3, local copies, waits for them, and re-layouts, place_rows(): gates[:, :, None] * values[:, None, :].astype(jnp.float32)  8.35 us
    reshape x2, local copies, waits for them, and re-layouts, on_device(): outgoing.reshape(experts_here, groups, capacity, features)  7.34 us
    scatter x1, other arithmetic, place_rows(): return outgoing.at[positions].set(scaled.reshape(-1, values.shape[1]))  6.88 us
    all_to_all x1, starting transfers between devices, on_device(): lax.all_to_all(jnp.stack([cotangent[0]] * lax.axis_size('tensor')), 'tens...  6.35 us
    all_to_all x1, waiting for transfers between devices, on_device(): lax.all_to_all(jnp.stack([cotangent[0]] * lax.axis_size('tensor')), 'tens...  4.65 us
    convert_element_type x1, local copies, waits for them, and re-layouts, on_device(): picked.astype(jnp.float32) * fore_gates[:, :, None]  4.61 us
  transfers between devices with their start and end apart: 6, of which 5 were waited for; matrix products, arithmetic and copies ran while one was open for 42% of the time, Pallas kernels for 0%

profile of v1, /device:TPU:0, one launch (start us, length us, event | category | flops | bytes accessed | tf_op | source)
XLA Modules:
  0.0 133.2 jit_solution(13930493637760905565)
XLA Ops:
  7.2 1.7 %stack.3 = bf16[4,64,640]{2,1,0:T(8,128)(2,1)} broadcast(bf16[64,640]{1,0:T(8,128)(2,1)} %bitcast.49), dimensions={1,2} | broadcast | bytes 409600 | tf_op jit(solution)/shard_map/stack | solution.py:72
  8.8 6.3 %all-to-all-start.1 = ((bf16[4,64,640]{2,1,0:T(8,128)(2,1)}), bf16[4,64,640]{2,1,0:T(8,128)(2,1)S(1)}, u32[]{:S(2)}, u32[]{:S(2)}) async-start(bf16[4,64,640]{2,1,0:T(8,128)(2,1)} %stack.3), calls=%async_computation.2 | async-start | bytes 655360 | tf_op jit(solution)/shard_map/all_to_all | solution.py:72
  15.9 3.2 %convolution_convert_fusion = bf16[3,4,43,2560]{3,2,1,0:T(8,128)(2,1)S(1)} fusion(bf16[1,3,256,2560]{3,2,1,0:T(8,128)(2,1)} %param.12, bf16[3,4,43,256]{3,1,2,0:T(4,128)(2,1)} %bitcast.46), kind=kOutput, calls=%fused_computation.3 | convolution fusion | flops 677652480 | bytes 6838272 | tf_op jit(solution)/shard_map/egmh,ehd->egmd/dot_general | solution.py:62
  19.1 1.8 %copy.51 = bf16[3,4,43,2560]{3,2,0,1:T(8,128)(2,1)} copy(bf16[3,4,43,2560]{3,2,1,0:T(8,128)(2,1)S(1)} %convolution_convert_fusion) | data formatting | bytes 5283840 | tf_op jit(solution)/shard_map/convert_element_type | solution.py:64
  20.9 4.7 %all-to-all-done.1 = bf16[4,64,640]{2,1,0:T(8,128)(2,1)S(1)} async-done(((bf16[4,64,640]{2,1,0:T(8,128)(2,1)}), bf16[4,64,640]{2,1,0:T(8,128)(2,1)S(1)}, u32[]{:S(2)}, u32[]{:S(2)}) %all-to-all-start.1) | async-done | bytes 327712 | tf_op jit(solution)/shard_map/all_to_all | solution.py:72
  26.3 3.7 %all-to-all-start = ((bf16[3,4,43,2560]{3,2,0,1:T(8,128)(2,1)}), bf16[3,4,43,2560]{3,2,0,1:T(8,128)(2,1)S(1)}, u32[]{:S(2)}, u32[]{:S(2)}) async-start(bf16[3,4,43,2560]{3,2,0,1:T(8,128)(2,1)} %copy.51), calls=%async_computation | async-start | bytes 5898240 | tf_op jit(solution)/shard_map/all_to_all | solution.py:65
  32.1 3.1 %mul.125 = f32[64,6,2560]{2,1,0:T(8,128)} broadcast(bf16[64,2560]{1,0:T(8,128)(2,1)S(1)} %bitcast.43), dimensions={0,2} | broadcast | bytes 4259840 | tf_op jit(solution)/shard_map/mul | solution.py:29
  35.1 5.2 %mul.126 = f32[384,2560]{1,0:T(8,128)} reshape(f32[64,6,2560]{2,1,0:T(8,128)} %mul.125) | data formatting | bytes 7864320 | tf_op jit(solution)/shard_map/mul | solution.py:29
  40.3 6.9 %scatter_custom_fusion = bf16[516,2560]{1,0:T(8,128)(2,1)} fusion(s32[384]{0:T(512)S(1)} %fusion.29, f32[384,2560]{1,0:T(8,128)} %mul.126, f32[384]{0:T(512)S(1)} %mul.123, bf16[]{:T(256)} %constant.32.clone.1), kind=kCustom, calls=%fused_computation.10 | custom fusion | flops 1966080 | bytes 6576130 | tf_op jit(solution)/shard_map/scatter | solution.py:31
  47.2 3.7 %reshape.227 = bf16[3,4,43,2560]{3,2,1,0:T(8,128)(2,1)} reshape(bf16[516,2560]{1,0:T(8,128)(2,1)} %scatter_custom_fusion) | data formatting | bytes 5283840 | tf_op jit(solution)/shard_map/reshape | solution.py:78
  50.9 3.6 %copy.66 = bf16[3,4,43,2560]{3,2,0,1:T(8,128)(2,1)} copy(bf16[3,4,43,2560]{3,2,1,0:T(8,128)(2,1)} %reshape.227) | data formatting | bytes 5283840 | tf_op jit(solution)/shard_map/reshape | solution.py:78
  54.5 16.5 %all-to-all-done = bf16[3,4,43,2560]{3,2,0,1:T(8,128)(2,1)S(1)} async-done(((bf16[3,4,43,2560]{3,2,0,1:T(8,128)(2,1)}), bf16[3,4,43,2560]{3,2,0,1:T(8,128)(2,1)S(1)}, u32[]{:S(2)}, u32[]{:S(2)}) %all-to-all-start) | async-done | bytes 2641952 | tf_op jit(solution)/shard_map/all_to_all | solution.py:65
  71.0 4.6 %all-to-all-start.2 = ((bf16[3,4,43,2560]{3,2,0,1:T(8,128)(2,1)}), bf16[3,4,43,2560]{3,2,0,1:T(8,128)(2,1)}, u32[]{:S(2)}, u32[]{:S(2)}) async-start(bf16[3,4,43,2560]{3,2,0,1:T(8,128)(2,1)} %copy.66), calls=%async_computation.3 | async-start | bytes 5898240 | tf_op jit(solution)/shard_map/all_to_all | solution.py:77
  76.8 1.9 %copy.52 = bf16[3,4,43,2560]{3,2,1,0:T(8,128)(2,1)} copy(bf16[3,4,43,2560]{3,2,0,1:T(8,128)(2,1)S(1)} %all-to-all-done) | data formatting | bytes 5283840 | tf_op jit(solution)/shard_map/all_to_all | solution.py:65
  78.7 2.4 %reshape.225 = bf16[516,2560]{1,0:T(8,128)(2,1)S(1)} reshape(bf16[3,4,43,2560]{3,2,1,0:T(8,128)(2,1)} %copy.52) | data formatting | bytes 5283840 | tf_op jit(solution)/shard_map/reshape | solution.py:66
  81.1 3.3 %gather_fusion = bf16[384,2560]{1,0:T(8,128)(2,1)} fusion(bf16[516,2560]{1,0:T(8,128)(2,1)S(1)} %reshape.225, s32[1024]{0:T(1024)S(1)} %pad_clamp_fusion), kind=kCustom, calls=%fused_computation | custom fusion | bytes 3933696 | tf_op jit(solution)/shard_map/gather | solution.py:66
  84.4 4.6 %reshape.228 = f32[64,6,2560]{2,1,0:T(8,128)} reshape(bf16[384,2560]{1,0:T(8,128)(2,1)} %gather_fusion) | data formatting | bytes 5898240 | tf_op jit(solution)/shard_map/convert_element_type | solution.py:67
  89.0 4.4 %multiply_reduce_fusion = f32[64,2560]{1,0:T(8,128)S(1)} fusion(f32[64,6,2560]{2,1,0:T(8,128)} %reshape.228, f32[64,6]{1,0:T(8,128)S(1)} %bitcast.47), kind=kLoop, calls=%fused_computation.2 | loop fusion | flops 1802240 | bytes 4589056 | tf_op jit(solution)/shard_map/reduce_sum | solution.py:67
  93.4 2.9 %convolution_add_fusion = f32[64,2560]{1,0:T(8,128)} fusion(f32[64,2560]{1,0:T(8,128)S(1)} %multiply_reduce_fusion, bf16[1,384,2560]{2,1,0:T(8,128)(2,1)} %all-gather.3.cloned.1.call-done, bf16[1,64,384]{2,1,0:T(8,128)(2,1)S(1)} %copy-done), kind=kOutput, calls=%fused_computation.8 | convolution fusion | flops 125992960 | bytes 3325952 | tf_op jit(solution)/shard_map/dot_general | solution.py:55
  96.4 14.0 %all-to-all-done.2 = bf16[3,4,43,2560]{3,2,0,1:T(8,128)(2,1)} async-done(((bf16[3,4,43,2560]{3,2,0,1:T(8,128)(2,1)}), bf16[3,4,43,2560]{3,2,0,1:T(8,128)(2,1)}, u32[]{:S(2)}, u32[]{:S(2)}) %all-to-all-start.2) | async-done | bytes 2641952 | tf_op jit(solution)/shard_map/all_to_all | solution.py:77
  110.4 4.5 %fusion.15 = bf16[1,3,4,43,256]{4,3,2,1,0:T(8,128)(2,1)S(1)} fusion(bf16[1,3,256,2560]{3,2,1,0:T(8,128)(2,1)} %param.12, bf16[3,4,43,2560]{3,2,0,1:T(8,128)(2,1)} %all-to-all-done.2), kind=kOutput, calls=%fused_computation.17 | convolution fusion | flops 676463616 | bytes 6838272 | tf_op jit(solution)/shard_map/egmd,ehd->egmh/dot_general | solution.py:84
  115.8 4.5 %reduce-scatter.2.cloned.1.call-done = f32[64,640]{1,0:T(8,128)} async-done(((f32[64,2560]{1,0:T(8,128)}), f32[64,640]{1,0:T(8,128)}) %reduce-scatter.2.cloned.1.call-update) | async-done | bytes 163856 | tf_op jit(solution)/shard_map/reduce_scatter | solution.py:68
  121.2 1.6 %collective-permute-start = (bf16[64,640]{1,0:T(8,128)(2,1)S(1)}, bf16[64,640]{1,0:T(8,128)(2,1)S(1)}, u32[]{:S(2)}, u32[]{:S(2)}) collective-permute-start(bf16[64,640]{1,0:T(8,128)(2,1)S(1)} %convert_element_type.40), channel_id=1, source_target_pairs={{0,16},{16,0},{1,17},{17,1},{2,18},{18,2},{3,19},{19,3},{4,20},{20... | collective-permute-start | bytes 245768 | tf_op jit(solution)/shard_map/ppermute | solution.py:10
  124.1 1.6 %collective-permute-done = bf16[64,640]{1,0:T(8,128)(2,1)S(1)} collective-permute-done((bf16[64,640]{1,0:T(8,128)(2,1)S(1)}, bf16[64,640]{1,0:T(8,128)(2,1)S(1)}, u32[]{:S(2)}, u32[]{:S(2)}) %collective-permute-start) | collective-permute-done | bytes 81952 | tf_op jit(solution)/shard_map/ppermute | solution.py:10
  (52 shorter events, 8.5 us)
Async XLA Ops:
  7.2 86.3 %copy-start = (bf16[1,64,384]{2,1,0:T(8,128)(2,1)S(1)}, bf16[1,64,384]{2,1,0:T(8,128)(2,1)}, u32[]{:S(2)}) copy-start(bf16[1,64,384]{2,1,0:T(8,128)(2,1)} %param.13) | copy-start | bytes 147460
  8.8 16.7 %all-to-all-start.1 = ((bf16[4,64,640]{2,1,0:T(8,128)(2,1)}), bf16[4,64,640]{2,1,0:T(8,128)(2,1)S(1)}, u32[]{:S(2)}, u32[]{:S(2)}) async-start(bf16[4,64,640]{2,1,0:T(8,128)(2,1)} %stack.3), calls=%async_computation.2 | async-start | bytes 655360 | tf_op jit(solution)/shard_map/all_to_all | solution.py:72
  15.2 78.2 %all-gather.3.cloned.1.call-start = ((), (), s32[]{:S(2)}) async-start(), calls=%async_computation.5 | async-start | bytes 2457600 | tf_op jit(solution)/shard_map/all_gather | solution.py:57
  20.9 9.1 %copy-start.3 = (s32[1,64,6]{1,0,2:T(1,128)S(1)}, s32[1,64,6]{1,0,2:T(1,128)}, u32[]{:S(2)}) copy-start(s32[1,64,6]{1,0,2:T(1,128)} %param.15) | copy-start | bytes 4612
  20.9 9.8 %copy-start.5 = (f32[1,64,6]{1,0,2:T(1,128)S(1)}, f32[1,64,6]{1,0,2:T(1,128)}, u32[]{:S(2)}) copy-start(f32[1,64,6]{1,0,2:T(1,128)} %param.16) | copy-start | bytes 4612
  25.5 0.7 copy-start.2
  26.3 44.7 %all-to-all-start = ((bf16[3,4,43,2560]{3,2,0,1:T(8,128)(2,1)}), bf16[3,4,43,2560]{3,2,0,1:T(8,128)(2,1)S(1)}, u32[]{:S(2)}, u32[]{:S(2)}) async-start(bf16[3,4,43,2560]{3,2,0,1:T(8,128)(2,1)} %copy.51), calls=%async_computation | async-start | bytes 5898240 | tf_op jit(solution)/shard_map/all_to_all | solution.py:65
  54.5 21.3 %copy-start.4 = (s32[1,64,6]{1,0,2:T(1,128)S(1)}, s32[1,64,6]{1,0,2:T(1,128)}, u32[]{:S(2)}) copy-start(s32[1,64,6]{1,0,2:T(1,128)} %param.9) | copy-start | bytes 4612
  54.5 22.0 %copy-start.6 = (f32[1,64,6]{1,0,2:T(1,128)S(1)}, f32[1,64,6]{1,0,2:T(1,128)}, u32[]{:S(2)}) copy-start(f32[1,64,6]{1,0,2:T(1,128)} %param.10) | copy-start | bytes 4612
  71.0 39.5 %all-to-all-start.2 = ((bf16[3,4,43,2560]{3,2,0,1:T(8,128)(2,1)}), bf16[3,4,43,2560]{3,2,0,1:T(8,128)(2,1)}, u32[]{:S(2)}, u32[]{:S(2)}) async-start(bf16[3,4,43,2560]{3,2,0,1:T(8,128)(2,1)} %copy.66), calls=%async_computation.3 | async-start | bytes 5898240 | tf_op jit(solution)/shard_map/all_to_all | solution.py:77
  75.6 44.7 %reduce-scatter.2.cloned.1.call-start = ((), (), s32[]{:S(2)}) async-start(), calls=%async_computation.4 | async-start | bytes 819200 | tf_op jit(solution)/shard_map/reduce_scatter | solution.py:68
  96.4 26.4 %copy-start.1 = (bf16[1,384,2560]{2,1,0:T(8,128)(2,1)S(1)}, bf16[1,384,2560]{2,1,0:T(8,128)(2,1)}, u32[]{:S(2)}) copy-start(bf16[1,384,2560]{2,1,0:T(8,128)(2,1)} %all-gather.3.cloned.1.call-done) | copy-start | bytes 5898244
  121.2 4.5 %collective-permute-start = (bf16[64,640]{1,0:T(8,128)(2,1)S(1)}, bf16[64,640]{1,0:T(8,128)(2,1)S(1)}, u32[]{:S(2)}, u32[]{:S(2)}) collective-permute-start(bf16[64,640]{1,0:T(8,128)(2,1)S(1)} %convert_element_type.40), channel_id=1, source_target_pairs={{0,16},{16,0},{1,17},{17,1},{2,18},{18,2},{3,19},{19,3},{4,20},{20... | collective-permute-start | bytes 245768 | tf_op jit(solution)/shard_map/ppermute | solution.py:10
Sparse Core Ops, SparseCore 0:
  17.6 29.5 all-gather.2
  96.5 23.7 reduce-scatter.1
